TPU v7x, 32 devices: a whole 2x2x4 slice. The times are simulated.
32 devices in a mesh: wl: 4 (over x, core), gx: 2 (over y), gy: 4 (over z).
Axes of the slice: x: 2, y: 2, z: 4, core: 2. Of those that a mesh axis runs over, the one named last changes fastest.
Arguments:
- forward_efield: float32 [4, 3, 64, 32, 128], P('wl', None, 'gx', 'gy'), may hold values from -6 to 6
- forward_hfield: float32 [4, 3, 64, 32, 128], P('wl', None, 'gx', 'gy'), may hold values from -6 to 6
- adjoint_efield: float32 [4, 3, 64, 32, 128], P('wl', None, 'gx', 'gy'), may hold values from -6 to 6
- adjoint_hfield: float32 [4, 3, 64, 32, 128], P('wl', None, 'gx', 'gy'), may hold values from -6 to 6
- background: float32 [64, 32, 128], P('gx', 'gy'), may hold values from 1 to 4
- design: float32 [8, 64, 32], P('wl', 'gx', 'gy'), may hold values from 1.5 to 6
- source_profile: float32 [4, 64, 32], P('wl', 'gx', 'gy'), may hold values from -24 to 24
- source_layer: int32 [4], P('wl'), may hold values from 4 to 59
- monitor_layer: int32 [4], P('wl'), may hold values from 76 to 123
Outputs:
- final_forward: float32 [4, 3, 64, 32, 128], P('wl', None, 'gx', 'gy')
- final_adjoint: float32 [4, 3, 64, 32, 128], P('wl', None, 'gx', 'gy')
- gradient: float32 [8, 64, 32], P('wl', 'gx', 'gy')
Inputs may be any that keep to these rules, and one draw needn't show every extreme that they name: `source_layer`: a z layer below the design slab. `monitor_layer`: a z layer above the design slab.
All inputs are finite; a program needn't handle non-finite values.
Results may differ from a plain program's by a relative error of at most 0.0001.
Values sent between devices are 32-bit elements; how exact they have to be, the bound alone decides.
No kernel may reach another device: no remote copies, remote signals or barrier semaphores. Data moves between devices by JAX's collectives and lax.ppermute only.
A program may use at most 64 MiB of HBM per device.

v0:
```python
import math
import jax
import jax.numpy as jnp
from jax import lax
from jax.sharding import PartitionSpec as P

Z0 = 64
STEPS = 3
time_step = 0.5


def shifted_2(block, axis, distance):
    devices = range(lax.axis_size(axis))
    route = [(i - distance, i) for i in devices if i - distance in devices]
    return lax.ppermute(block, axis, route)


def neighbours(stacked, upward):
    offset = -1 if upward else 1
    plane_x = stacked[:, :1] if upward else stacked[:, -1:]
    plane_y = stacked[:, :, :1] if upward else stacked[:, :, -1:]
    got_x = shifted_2(plane_x, "gx", offset)
    got_y = shifted_2(plane_y, "gy", offset)
    return (got_x, got_y)


def along(stacked, axis, edge, upward):
    count = stacked.shape[axis]
    if upward:
        shifted = jnp.concatenate([lax.slice_in_dim(stacked, 1, count, axis=axis), edge], axis=axis)
        return shifted - stacked
    shifted = jnp.concatenate([edge, lax.slice_in_dim(stacked, 0, count - 1, axis=axis)], axis=axis)
    return stacked - shifted


def curl(stacked, upward):
    comps, width, height, depth = stacked.shape
    edge_x, edge_y = neighbours(stacked, upward)
    edge_z = jnp.zeros((comps, width, height, 1), jnp.float32)
    along_x = along(stacked, 1, edge_x, upward)
    along_y = along(stacked, 2, edge_y, upward)
    along_z = along(stacked, 3, edge_z, upward)
    return jnp.stack([along_y[2] - along_z[1], along_z[0] - along_x[2], along_x[1] - along_y[0]])


def run_window(efield, hfield, adj_e, adj_h, coef, source_term, omega, monitor_mask, slab_depth):
    slabs = []
    monitors = []
    monitor_pick = monitor_mask[None, None, None, :]
    for turn in range(STEPS):
        hfield = hfield - time_step * curl(efield, True)
        efield = efield + coef * curl(hfield, False)
        signal = jnp.sin(omega * ((turn + 1) * time_step))
        efield = efield.at[0].add(time_step * signal * source_term)
        slabs.append(efield[:, :, :, Z0 : Z0 + slab_depth])
        monitors.append(jnp.sum(efield * monitor_pick, axis=3, keepdims=True))
    total = jnp.zeros((efield.shape[1], efield.shape[2], slab_depth), jnp.float32)
    for turn in range(STEPS):
        adj_h = adj_h - time_step * curl(adj_e, True)
        adj_e = adj_e + coef * curl(adj_h, False)
        adj_e = adj_e + 2.0 * time_step * monitors[STEPS - 1 - turn] * monitor_mask
        total = total + jnp.sum(
            slabs[STEPS - 1 - turn] * adj_e[:, :, :, Z0 : Z0 + slab_depth], axis=0
        )
    return (efield, adj_e, total)


def per_device(
    forward_efield,
    forward_hfield,
    adjoint_efield,
    adjoint_hfield,
    background,
    design,
    source_profile,
    source_layer,
    monitor_layer,
):
    groups = lax.axis_size("wl")
    owned = design.shape[0]
    slab_depth = owned * groups
    depth = background.shape[2]
    tiles = lax.all_gather(design, "wl", axis=0, tiled=True)
    permit = jnp.concatenate(
        [
            background[:, :, :Z0],
            jnp.transpose(tiles, (1, 2, 0)),
            background[:, :, Z0 + slab_depth :],
        ],
        axis=2,
    )
    layers = lax.iota(jnp.int32, depth)
    wave_index = lax.axis_index("wl").astype(jnp.float32)
    omega = jnp.float32(2.0 * math.pi) / (16.0 + 32.0 * wave_index / groups)
    source_mask = (layers == source_layer[0]).astype(jnp.float32)
    monitor_mask = (layers == monitor_layer[0]).astype(jnp.float32)
    source_term = source_profile[0][:, :, None] * source_mask
    coef = time_step / permit
    efield, adj_e, total = run_window(
        forward_efield[0],
        forward_hfield[0],
        adjoint_efield[0],
        adjoint_hfield[0],
        coef,
        source_term,
        omega,
        monitor_mask,
        slab_depth,
    )
    local_grad = jnp.transpose(omega * omega * total, (2, 0, 1))
    summed = lax.psum(local_grad, "wl")
    gradient = lax.dynamic_slice_in_dim(summed, lax.axis_index("wl") * owned, owned, 0)
    return (efield[None], adj_e[None], gradient)


def solution(mesh):
    return jax.shard_map(
        per_device,
        mesh=mesh,
        in_specs=(
            P("wl", None, "gx", "gy", None),
            P("wl", None, "gx", "gy", None),
            P("wl", None, "gx", "gy", None),
            P("wl", None, "gx", "gy", None),
            P("gx", "gy", None),
            P("wl", "gx", "gy"),
            P("wl", "gx", "gy"),
            P("wl"),
            P("wl"),
        ),
        out_specs=(
            P("wl", None, "gx", "gy", None),
            P("wl", None, "gx", "gy", None),
            P("wl", "gx", "gy"),
        ),
        check_vma=False,
    )
```

profile of v0, /device:TPU:0, one launch (start us, length us, event | category | flops | bytes accessed | tf_op | source)
XLA Modules:
  0.0 120.3 jit_solution(9037135590626028653)
XLA Ops:
  0.6 1.0 slice.645
  1.7 1.3 %collective-permute-start = (f32[3,32,1,128]{3,2,1,0:T(1,128)S(1)}, f32[3,32,1,128]{3,2,1,0:T(1,128)S(1)}, u32[]{:S(2)}, u32[]{:S(2)}) collective-permute-start(f32[3,32,1,128]{3,2,1,0:T(1,128)S(1)} %slice.645), channel_id=1, source_target_pairs={{1,0},{2,1},{3,2},{5,4},{6,5},{7,6},{9,8},{10,9},{11,10},{13,12},{... | collective-permute-start | bytes 147464 | tf_op jit(solution)/shard_map/ppermute | solution.py:15
  3.0 0.7 slice.651
  3.7 1.3 %collective-permute-start.1 = (f32[3,1,8,128]{3,2,1,0:T(8,128)S(1)}, f32[3,1,8,128]{3,2,1,0:T(8,128)S(1)}, u32[]{:S(2)}, u32[]{:S(2)}) collective-permute-start(f32[3,1,8,128]{3,2,1,0:T(8,128)S(1)} %slice.651), channel_id=1, source_target_pairs={{4,0},{5,1},{6,2},{7,3},{12,8},{13,9},{14,10},{15,11},{20,16},{21,... | collective-permute-start | bytes 36872 | tf_op jit(solution)/shard_map/ppermute | solution.py:15
  5.0 1.0 slice.714
  6.0 1.4 %collective-permute-start.12 = (f32[3,32,1,128]{3,2,1,0:T(1,128)S(1)}, f32[3,32,1,128]{3,2,1,0:T(1,128)S(1)}, u32[]{:S(2)}, u32[]{:S(2)}) collective-permute-start(f32[3,32,1,128]{3,2,1,0:T(1,128)S(1)} %slice.714), channel_id=1, source_target_pairs={{1,0},{2,1},{3,2},{5,4},{6,5},{7,6},{9,8},{10,9},{11,10},{13,12},{... | collective-permute-start | bytes 147464 | tf_op jit(solution)/shard_map/ppermute | solution.py:15
  7.4 0.7 slice.720
  8.2 1.3 %collective-permute-start.13 = (f32[3,1,8,128]{3,2,1,0:T(8,128)S(1)}, f32[3,1,8,128]{3,2,1,0:T(8,128)S(1)}, u32[]{:S(2)}, u32[]{:S(2)}) collective-permute-start(f32[3,1,8,128]{3,2,1,0:T(8,128)S(1)} %slice.720), channel_id=1, source_target_pairs={{4,0},{5,1},{6,2},{7,3},{12,8},{13,9},{14,10},{15,11},{20,16},{21,... | collective-permute-start | bytes 36872 | tf_op jit(solution)/shard_map/ppermute | solution.py:15
  9.5 6.2 %all_gather.3 = f32[8,32,8]{1,2,0:T(8,128)S(1)} all-gather(f32[2,32,8]{1,2,0:T(8,128)S(1)} %copy-done.26), channel_id=1, replica_groups=mesh['wl'=4,'gx'=2,'gy'=4] {'wl'}, dimensions={0}, use_global_device_ids=true | all-gather | bytes 10240 | tf_op jit(solution)/shard_map/all_gather | solution.py:83
  17.4 0.2 slice.647
  17.6 1.0 copy-done
  19.1 0.6 copy-done.27
  20.1 0.9 copy-done.1
  21.1 5.2 %collective-permute-start.2 = (f32[3,32,1,128]{3,2,1,0:T(1,128)S(1)}, f32[3,32,1,128]{3,2,1,0:T(1,128)S(1)}, u32[]{:S(2)}, u32[]{:S(2)}) collective-permute-start(f32[3,32,1,128]{3,2,1,0:T(1,128)S(1)} %slice.655), channel_id=1, source_target_pairs={{0,1},{1,2},{2,3},{4,5},{5,6},{6,7},{8,9},{9,10},{10,11},{12,13},{... | collective-permute-start | bytes 147464 | tf_op jit(solution)/shard_map/ppermute | solution.py:15
  26.3 4.5 %collective-permute-start.3 = (f32[3,1,8,128]{3,2,1,0:T(8,128)S(1)}, f32[3,1,8,128]{3,2,1,0:T(8,128)S(1)}, u32[]{:S(2)}, u32[]{:S(2)}) collective-permute-start(f32[3,1,8,128]{3,2,1,0:T(8,128)S(1)} %slice.661), channel_id=1, source_target_pairs={{0,4},{1,5},{2,6},{3,7},{8,12},{9,13},{10,14},{11,15},{16,20},{17,... | collective-permute-start | bytes 36872 | tf_op jit(solution)/shard_map/ppermute | solution.py:15
  31.1 1.2 collective-permute-done.3
  32.3 0.2 pad_subtract_fusion.10
  32.7 1.3 %collective-permute-start.4 = (f32[3,32,1,128]{3,2,1,0:T(1,128)S(1)}, f32[3,32,1,128]{3,2,1,0:T(1,128)S(1)}, u32[]{:S(2)}, u32[]{:S(2)}) collective-permute-start(f32[3,32,1,128]{3,2,1,0:T(1,128)S(1)} %slice.668), channel_id=1, source_target_pairs={{1,0},{2,1},{3,2},{5,4},{6,5},{7,6},{9,8},{10,9},{11,10},{13,12},{... | collective-permute-start | bytes 147464 | tf_op jit(solution)/shard_map/ppermute | solution.py:15
  34.0 1.3 %collective-permute-start.5 = (f32[3,1,8,128]{3,2,1,0:T(8,128)S(1)}, f32[3,1,8,128]{3,2,1,0:T(8,128)S(1)}, u32[]{:S(2)}, u32[]{:S(2)}) collective-permute-start(f32[3,1,8,128]{3,2,1,0:T(8,128)S(1)} %slice.674), channel_id=1, source_target_pairs={{4,0},{5,1},{6,2},{7,3},{12,8},{13,9},{14,10},{15,11},{20,16},{21,... | collective-permute-start | bytes 36872 | tf_op jit(solution)/shard_map/ppermute | solution.py:15
  35.4 0.2 slice.670
  35.6 4.0 %collective-permute-done.5 = f32[3,1,8,128]{3,2,1,0:T(8,128)S(1)} collective-permute-done((f32[3,1,8,128]{3,2,1,0:T(8,128)S(1)}, f32[3,1,8,128]{3,2,1,0:T(8,128)S(1)}, u32[]{:S(2)}, u32[]{:S(2)}) %collective-permute-start.5) | collective-permute-done | bytes 12320 | tf_op jit(solution)/shard_map/ppermute | solution.py:15
  40.0 4.6 %collective-permute-start.6 = (f32[3,32,1,128]{3,2,1,0:T(1,128)S(1)}, f32[3,32,1,128]{3,2,1,0:T(1,128)S(1)}, u32[]{:S(2)}, u32[]{:S(2)}) collective-permute-start(f32[3,32,1,128]{3,2,1,0:T(1,128)S(1)} %slice.678), channel_id=1, source_target_pairs={{0,1},{1,2},{2,3},{4,5},{5,6},{6,7},{8,9},{9,10},{10,11},{12,13},{... | collective-permute-start | bytes 147464 | tf_op jit(solution)/shard_map/ppermute | solution.py:15
  44.5 2.7 %collective-permute-start.7 = (f32[3,1,8,128]{3,2,1,0:T(8,128)S(1)}, f32[3,1,8,128]{3,2,1,0:T(8,128)S(1)}, u32[]{:S(2)}, u32[]{:S(2)}) collective-permute-start(f32[3,1,8,128]{3,2,1,0:T(8,128)S(1)} %slice.684), channel_id=1, source_target_pairs={{0,4},{1,5},{2,6},{3,7},{8,12},{9,13},{10,14},{11,15},{16,20},{17,... | collective-permute-start | bytes 36872 | tf_op jit(solution)/shard_map/ppermute | solution.py:15
  47.4 3.9 %collective-permute-start.14 = (f32[3,32,1,128]{3,2,1,0:T(1,128)S(1)}, f32[3,32,1,128]{3,2,1,0:T(1,128)S(1)}, u32[]{:S(2)}, u32[]{:S(2)}) collective-permute-start(f32[3,32,1,128]{3,2,1,0:T(1,128)S(1)} %slice.724), channel_id=1, source_target_pairs={{0,1},{1,2},{2,3},{4,5},{5,6},{6,7},{8,9},{9,10},{10,11},{12,13},{... | collective-permute-start | bytes 147464 | tf_op jit(solution)/shard_map/ppermute | solution.py:15
  51.3 1.3 %collective-permute-start.15 = (f32[3,1,8,128]{3,2,1,0:T(8,128)S(1)}, f32[3,1,8,128]{3,2,1,0:T(8,128)S(1)}, u32[]{:S(2)}, u32[]{:S(2)}) collective-permute-start(f32[3,1,8,128]{3,2,1,0:T(8,128)S(1)} %slice.730), channel_id=1, source_target_pairs={{0,4},{1,5},{2,6},{3,7},{8,12},{9,13},{10,14},{11,15},{16,20},{17,... | collective-permute-start | bytes 36872 | tf_op jit(solution)/shard_map/ppermute | solution.py:15
  52.6 0.2 pad_subtract_fusion.8
  53.1 1.3 %collective-permute-start.8 = (f32[3,32,1,128]{3,2,1,0:T(1,128)S(1)}, f32[3,32,1,128]{3,2,1,0:T(1,128)S(1)}, u32[]{:S(2)}, u32[]{:S(2)}) collective-permute-start(f32[3,32,1,128]{3,2,1,0:T(1,128)S(1)} %slice.691), channel_id=1, source_target_pairs={{1,0},{2,1},{3,2},{5,4},{6,5},{7,6},{9,8},{10,9},{11,10},{13,12},{... | collective-permute-start | bytes 147464 | tf_op jit(solution)/shard_map/ppermute | solution.py:15
  54.4 1.3 %collective-permute-start.9 = (f32[3,1,8,128]{3,2,1,0:T(8,128)S(1)}, f32[3,1,8,128]{3,2,1,0:T(8,128)S(1)}, u32[]{:S(2)}, u32[]{:S(2)}) collective-permute-start(f32[3,1,8,128]{3,2,1,0:T(8,128)S(1)} %slice.697), channel_id=1, source_target_pairs={{4,0},{5,1},{6,2},{7,3},{12,8},{13,9},{14,10},{15,11},{20,16},{21,... | collective-permute-start | bytes 36872 | tf_op jit(solution)/shard_map/ppermute | solution.py:15
  55.8 0.2 pad_subtract_fusion.4
  56.2 3.8 %collective-permute-done.9 = f32[3,1,8,128]{3,2,1,0:T(8,128)S(1)} collective-permute-done((f32[3,1,8,128]{3,2,1,0:T(8,128)S(1)}, f32[3,1,8,128]{3,2,1,0:T(8,128)S(1)}, u32[]{:S(2)}, u32[]{:S(2)}) %collective-permute-start.9) | collective-permute-done | bytes 12320 | tf_op jit(solution)/shard_map/ppermute | solution.py:15
  60.4 4.5 %collective-permute-start.10 = (f32[3,32,1,128]{3,2,1,0:T(1,128)S(1)}, f32[3,32,1,128]{3,2,1,0:T(1,128)S(1)}, u32[]{:S(2)}, u32[]{:S(2)}) collective-permute-start(f32[3,32,1,128]{3,2,1,0:T(1,128)S(1)} %slice.701), channel_id=1, source_target_pairs={{0,1},{1,2},{2,3},{4,5},{5,6},{6,7},{8,9},{9,10},{10,11},{12,13},{... | collective-permute-start | bytes 147464 | tf_op jit(solution)/shard_map/ppermute | solution.py:15
  64.9 1.6 %collective-permute-start.11 = (f32[3,1,8,128]{3,2,1,0:T(8,128)S(1)}, f32[3,1,8,128]{3,2,1,0:T(8,128)S(1)}, u32[]{:S(2)}, u32[]{:S(2)}) collective-permute-start(f32[3,1,8,128]{3,2,1,0:T(8,128)S(1)} %slice.707), channel_id=1, source_target_pairs={{0,4},{1,5},{2,6},{3,7},{8,12},{9,13},{10,14},{11,15},{16,20},{17,... | collective-permute-start | bytes 36872 | tf_op jit(solution)/shard_map/ppermute | solution.py:15
  66.7 1.3 %collective-permute-done.11 = f32[3,1,8,128]{3,2,1,0:T(8,128)S(1)} collective-permute-done((f32[3,1,8,128]{3,2,1,0:T(8,128)S(1)}, f32[3,1,8,128]{3,2,1,0:T(8,128)S(1)}, u32[]{:S(2)}, u32[]{:S(2)}) %collective-permute-start.11) | collective-permute-done | bytes 12320 | tf_op jit(solution)/shard_map/ppermute | solution.py:15
  68.0 0.3 pad_subtract_fusion.6
  68.5 0.8 multiply_reduce_fusion
  69.3 0.2 fusion.21
  69.5 1.3 %collective-permute-start.16 = (f32[3,32,1,128]{3,2,1,0:T(1,128)S(1)}, f32[3,32,1,128]{3,2,1,0:T(1,128)S(1)}, u32[]{:S(2)}, u32[]{:S(2)}) collective-permute-start(f32[3,32,1,128]{3,2,1,0:T(1,128)S(1)} %slice.736), channel_id=1, source_target_pairs={{1,0},{2,1},{3,2},{5,4},{6,5},{7,6},{9,8},{10,9},{11,10},{13,12},{... | collective-permute-start | bytes 147464 | tf_op jit(solution)/shard_map/ppermute | solution.py:15
  70.8 1.3 %collective-permute-start.17 = (f32[3,1,8,128]{3,2,1,0:T(8,128)S(1)}, f32[3,1,8,128]{3,2,1,0:T(8,128)S(1)}, u32[]{:S(2)}, u32[]{:S(2)}) collective-permute-start(f32[3,1,8,128]{3,2,1,0:T(8,128)S(1)} %slice.742), channel_id=1, source_target_pairs={{4,0},{5,1},{6,2},{7,3},{12,8},{13,9},{14,10},{15,11},{20,16},{21,... | collective-permute-start | bytes 36872 | tf_op jit(solution)/shard_map/ppermute | solution.py:15
  72.4 4.0 %collective-permute-done.17 = f32[3,1,8,128]{3,2,1,0:T(8,128)S(1)} collective-permute-done((f32[3,1,8,128]{3,2,1,0:T(8,128)S(1)}, f32[3,1,8,128]{3,2,1,0:T(8,128)S(1)}, u32[]{:S(2)}, u32[]{:S(2)}) %collective-permute-start.17) | collective-permute-done | bytes 12320 | tf_op jit(solution)/shard_map/ppermute | solution.py:15
  76.4 0.2 pad_subtract_fusion.3
  76.9 4.5 %collective-permute-start.18 = (f32[3,32,1,128]{3,2,1,0:T(1,128)S(1)}, f32[3,32,1,128]{3,2,1,0:T(1,128)S(1)}, u32[]{:S(2)}, u32[]{:S(2)}) collective-permute-start(f32[3,32,1,128]{3,2,1,0:T(1,128)S(1)} %slice.746), channel_id=1, source_target_pairs={{0,1},{1,2},{2,3},{4,5},{5,6},{6,7},{8,9},{9,10},{10,11},{12,13},{... | collective-permute-start | bytes 147464 | tf_op jit(solution)/shard_map/ppermute | solution.py:15
  81.4 1.6 %collective-permute-start.19 = (f32[3,1,8,128]{3,2,1,0:T(8,128)S(1)}, f32[3,1,8,128]{3,2,1,0:T(8,128)S(1)}, u32[]{:S(2)}, u32[]{:S(2)}) collective-permute-start(f32[3,1,8,128]{3,2,1,0:T(8,128)S(1)} %slice.752), channel_id=1, source_target_pairs={{0,4},{1,5},{2,6},{3,7},{8,12},{9,13},{10,14},{11,15},{16,20},{17,... | collective-permute-start | bytes 36872 | tf_op jit(solution)/shard_map/ppermute | solution.py:15
  83.1 1.4 %collective-permute-done.19 = f32[3,1,8,128]{3,2,1,0:T(8,128)S(1)} collective-permute-done((f32[3,1,8,128]{3,2,1,0:T(8,128)S(1)}, f32[3,1,8,128]{3,2,1,0:T(8,128)S(1)}, u32[]{:S(2)}, u32[]{:S(2)}) %collective-permute-start.19) | collective-permute-done | bytes 12320 | tf_op jit(solution)/shard_map/ppermute | solution.py:15
  84.5 0.2 pad_subtract_fusion.2
  84.8 0.3 fusion.24
  85.1 0.3 copy-done.8
  85.5 0.6 slice.758
  86.1 1.3 %collective-permute-start.20 = (f32[3,32,1,128]{3,2,1,0:T(1,128)}, f32[3,32,1,128]{3,2,1,0:T(1,128)}, u32[]{:S(2)}, u32[]{:S(2)}) collective-permute-start(f32[3,32,1,128]{3,2,1,0:T(1,128)} %slice.758), channel_id=1, source_target_pairs={{1,0},{2,1},{3,2},{5,4},{6,5},{7,6},{9,8},{10,9},{11,10},{13,12},{... | collective-permute-start | bytes 147464 | tf_op jit(solution)/shard_map/ppermute | solution.py:15
  87.4 1.3 %collective-permute-start.21 = (f32[3,1,8,128]{3,2,1,0:T(8,128)S(1)}, f32[3,1,8,128]{3,2,1,0:T(8,128)}, u32[]{:S(2)}, u32[]{:S(2)}) collective-permute-start(f32[3,1,8,128]{3,2,1,0:T(8,128)S(1)} %slice.764), channel_id=1, source_target_pairs={{4,0},{5,1},{6,2},{7,3},{12,8},{13,9},{14,10},{15,11},{20,16},{21,... | collective-permute-start | bytes 36872 | tf_op jit(solution)/shard_map/ppermute | solution.py:15
  88.7 0.8 slice.784
  89.5 0.6 slice.786
  90.4 2.8 %collective-permute-done.21 = f32[3,1,8,128]{3,2,1,0:T(8,128)} collective-permute-done((f32[3,1,8,128]{3,2,1,0:T(8,128)S(1)}, f32[3,1,8,128]{3,2,1,0:T(8,128)}, u32[]{:S(2)}, u32[]{:S(2)}) %collective-permute-start.21) | collective-permute-done | bytes 12320 | tf_op jit(solution)/shard_map/ppermute | solution.py:15
  93.2 1.2 pad_subtract_fusion.1
  94.4 0.8 copy-done.7
  95.4 4.5 %collective-permute-start.22 = (f32[3,32,1,128]{3,2,1,0:T(1,128)S(1)}, f32[3,32,1,128]{3,2,1,0:T(1,128)S(1)}, u32[]{:S(2)}, u32[]{:S(2)}) collective-permute-start(f32[3,32,1,128]{3,2,1,0:T(1,128)S(1)} %slice.768), channel_id=1, source_target_pairs={{0,1},{1,2},{2,3},{4,5},{5,6},{6,7},{8,9},{9,10},{10,11},{12,13},{... | collective-permute-start | bytes 147464 | tf_op jit(solution)/shard_map/ppermute | solution.py:15
  100.0 3.3 %collective-permute-start.23 = (f32[3,1,8,128]{3,2,1,0:T(8,128)S(1)}, f32[3,1,8,128]{3,2,1,0:T(8,128)S(1)}, u32[]{:S(2)}, u32[]{:S(2)}) collective-permute-start(f32[3,1,8,128]{3,2,1,0:T(8,128)S(1)} %slice.774), channel_id=1, source_target_pairs={{0,4},{1,5},{2,6},{3,7},{8,12},{9,13},{10,14},{11,15},{16,20},{17,... | collective-permute-start | bytes 36872 | tf_op jit(solution)/shard_map/ppermute | solution.py:15
  103.3 0.3 fusion.6
  103.6 1.1 collective-permute-done.23
  104.7 0.3 pad_subtract_fusion
  105.0 0.8 copy-done.23
  105.8 0.6 fusion.5
  106.5 11.6 %psum.7 = f32[8,32,8]{0,2,1:T(8,128)S(1)} all-reduce(f32[8,32,8]{0,2,1:T(8,128)S(1)} %multiply_bitcast_fusion), channel_id=1, replica_groups=mesh['wl'=4,'gx'=2,'gy'=4] {'wl'}, use_global_device_ids=true, to_apply=%region_6.0 | all-reduce | flops 2048 | bytes 16384 | tf_op jit(solution)/shard_map/psum | solution.py:111
  118.2 0.7 copy.16
  119.1 1.1 fusion.19
  (145 shorter events, 4.6 us)
Async XLA Ops:
  1.7 18.2 %collective-permute-start = (f32[3,32,1,128]{3,2,1,0:T(1,128)S(1)}, f32[3,32,1,128]{3,2,1,0:T(1,128)S(1)}, u32[]{:S(2)}, u32[]{:S(2)}) collective-permute-start(f32[3,32,1,128]{3,2,1,0:T(1,128)S(1)} %slice.645), channel_id=1, source_target_pairs={{1,0},{2,1},{3,2},{5,4},{6,5},{7,6},{9,8},{10,9},{11,10},{13,12},{... | collective-permute-start | bytes 147464 | tf_op jit(solution)/shard_map/ppermute | solution.py:15
  3.7 16.2 %collective-permute-start.1 = (f32[3,1,8,128]{3,2,1,0:T(8,128)S(1)}, f32[3,1,8,128]{3,2,1,0:T(8,128)S(1)}, u32[]{:S(2)}, u32[]{:S(2)}) collective-permute-start(f32[3,1,8,128]{3,2,1,0:T(8,128)S(1)} %slice.651), channel_id=1, source_target_pairs={{4,0},{5,1},{6,2},{7,3},{12,8},{13,9},{14,10},{15,11},{20,16},{21,... | collective-permute-start | bytes 36872 | tf_op jit(solution)/shard_map/ppermute | solution.py:15
  5.0 4.5 %copy-start.26 = (f32[2,32,8]{1,2,0:T(8,128)S(1)}, f32[2,32,8]{1,2,0:T(8,128)}, u32[]{:S(2)}) copy-start(f32[2,32,8]{1,2,0:T(8,128)} %param.20) | copy-start | bytes 6148
  6.0 9.8 %copy-start.24 = (f32[32,8,128]{2,1,0:T(8,128)S(1)}, f32[32,8,128]{2,1,0:T(8,128)}, u32[]{:S(2)}) copy-start(f32[32,8,128]{2,1,0:T(8,128)} %param.19) | copy-start | bytes 393220
  6.0 24.9 %collective-permute-start.12 = (f32[3,32,1,128]{3,2,1,0:T(1,128)S(1)}, f32[3,32,1,128]{3,2,1,0:T(1,128)S(1)}, u32[]{:S(2)}, u32[]{:S(2)}) collective-permute-start(f32[3,32,1,128]{3,2,1,0:T(1,128)S(1)} %slice.714), channel_id=1, source_target_pairs={{1,0},{2,1},{3,2},{5,4},{6,5},{7,6},{9,8},{10,9},{11,10},{13,12},{... | collective-permute-start | bytes 147464 | tf_op jit(solution)/shard_map/ppermute | solution.py:15
  8.2 22.7 %collective-permute-start.13 = (f32[3,1,8,128]{3,2,1,0:T(8,128)S(1)}, f32[3,1,8,128]{3,2,1,0:T(8,128)S(1)}, u32[]{:S(2)}, u32[]{:S(2)}) collective-permute-start(f32[3,1,8,128]{3,2,1,0:T(8,128)S(1)} %slice.720), channel_id=1, source_target_pairs={{4,0},{5,1},{6,2},{7,3},{12,8},{13,9},{14,10},{15,11},{20,16},{21,... | collective-permute-start | bytes 36872 | tf_op jit(solution)/shard_map/ppermute | solution.py:15
  15.8 1.6 %copy-start.3 = (f32[1,3,32,8,128]{4,3,2,1,0:T(8,128)S(1)}, f32[1,3,32,8,128]{4,3,2,1,0:T(8,128)}, u32[]{:S(2)}) copy-start(f32[1,3,32,8,128]{4,3,2,1,0:T(8,128)} %param.15) | copy-start | bytes 1179652
  17.6 1.0 copy-start
  19.0 0.7 copy-start.27
  20.0 1.0 copy-start.1
  21.1 11.2 %collective-permute-start.2 = (f32[3,32,1,128]{3,2,1,0:T(1,128)S(1)}, f32[3,32,1,128]{3,2,1,0:T(1,128)S(1)}, u32[]{:S(2)}, u32[]{:S(2)}) collective-permute-start(f32[3,32,1,128]{3,2,1,0:T(1,128)S(1)} %slice.655), channel_id=1, source_target_pairs={{0,1},{1,2},{2,3},{4,5},{5,6},{6,7},{8,9},{9,10},{10,11},{12,13},{... | collective-permute-start | bytes 147464 | tf_op jit(solution)/shard_map/ppermute | solution.py:15
  26.3 5.9 %collective-permute-start.3 = (f32[3,1,8,128]{3,2,1,0:T(8,128)S(1)}, f32[3,1,8,128]{3,2,1,0:T(8,128)S(1)}, u32[]{:S(2)}, u32[]{:S(2)}) collective-permute-start(f32[3,1,8,128]{3,2,1,0:T(8,128)S(1)} %slice.661), channel_id=1, source_target_pairs={{0,4},{1,5},{2,6},{3,7},{8,12},{9,13},{10,14},{11,15},{16,20},{17,... | collective-permute-start | bytes 36872 | tf_op jit(solution)/shard_map/ppermute | solution.py:15
  32.7 6.9 %collective-permute-start.4 = (f32[3,32,1,128]{3,2,1,0:T(1,128)S(1)}, f32[3,32,1,128]{3,2,1,0:T(1,128)S(1)}, u32[]{:S(2)}, u32[]{:S(2)}) collective-permute-start(f32[3,32,1,128]{3,2,1,0:T(1,128)S(1)} %slice.668), channel_id=1, source_target_pairs={{1,0},{2,1},{3,2},{5,4},{6,5},{7,6},{9,8},{10,9},{11,10},{13,12},{... | collective-permute-start | bytes 147464 | tf_op jit(solution)/shard_map/ppermute | solution.py:15
  34.0 5.6 %collective-permute-start.5 = (f32[3,1,8,128]{3,2,1,0:T(8,128)S(1)}, f32[3,1,8,128]{3,2,1,0:T(8,128)S(1)}, u32[]{:S(2)}, u32[]{:S(2)}) collective-permute-start(f32[3,1,8,128]{3,2,1,0:T(8,128)S(1)} %slice.674), channel_id=1, source_target_pairs={{4,0},{5,1},{6,2},{7,3},{12,8},{13,9},{14,10},{15,11},{20,16},{21,... | collective-permute-start | bytes 36872 | tf_op jit(solution)/shard_map/ppermute | solution.py:15
  39.8 7.4 %copy-start.2 = (f32[1,3,32,8,128]{4,3,2,1,0:T(8,128)S(1)}, f32[1,3,32,8,128]{4,3,2,1,0:T(8,128)}, u32[]{:S(2)}) copy-start(f32[1,3,32,8,128]{4,3,2,1,0:T(8,128)} %param.18) | copy-start | bytes 1179652
  40.0 12.7 %collective-permute-start.6 = (f32[3,32,1,128]{3,2,1,0:T(1,128)S(1)}, f32[3,32,1,128]{3,2,1,0:T(1,128)S(1)}, u32[]{:S(2)}, u32[]{:S(2)}) collective-permute-start(f32[3,32,1,128]{3,2,1,0:T(1,128)S(1)} %slice.678), channel_id=1, source_target_pairs={{0,1},{1,2},{2,3},{4,5},{5,6},{6,7},{8,9},{9,10},{10,11},{12,13},{... | collective-permute-start | bytes 147464 | tf_op jit(solution)/shard_map/ppermute | solution.py:15
  44.5 8.1 %collective-permute-start.7 = (f32[3,1,8,128]{3,2,1,0:T(8,128)S(1)}, f32[3,1,8,128]{3,2,1,0:T(8,128)S(1)}, u32[]{:S(2)}, u32[]{:S(2)}) collective-permute-start(f32[3,1,8,128]{3,2,1,0:T(8,128)S(1)} %slice.684), channel_id=1, source_target_pairs={{0,4},{1,5},{2,6},{3,7},{8,12},{9,13},{10,14},{11,15},{16,20},{17,... | collective-permute-start | bytes 36872 | tf_op jit(solution)/shard_map/ppermute | solution.py:15
  47.4 8.4 %collective-permute-start.14 = (f32[3,32,1,128]{3,2,1,0:T(1,128)S(1)}, f32[3,32,1,128]{3,2,1,0:T(1,128)S(1)}, u32[]{:S(2)}, u32[]{:S(2)}) collective-permute-start(f32[3,32,1,128]{3,2,1,0:T(1,128)S(1)} %slice.724), channel_id=1, source_target_pairs={{0,1},{1,2},{2,3},{4,5},{5,6},{6,7},{8,9},{9,10},{10,11},{12,13},{... | collective-permute-start | bytes 147464 | tf_op jit(solution)/shard_map/ppermute | solution.py:15
  51.3 4.5 %collective-permute-start.15 = (f32[3,1,8,128]{3,2,1,0:T(8,128)S(1)}, f32[3,1,8,128]{3,2,1,0:T(8,128)S(1)}, u32[]{:S(2)}, u32[]{:S(2)}) collective-permute-start(f32[3,1,8,128]{3,2,1,0:T(8,128)S(1)} %slice.730), channel_id=1, source_target_pairs={{0,4},{1,5},{2,6},{3,7},{8,12},{9,13},{10,14},{11,15},{16,20},{17,... | collective-permute-start | bytes 36872 | tf_op jit(solution)/shard_map/ppermute | solution.py:15
  53.1 6.9 %collective-permute-start.8 = (f32[3,32,1,128]{3,2,1,0:T(1,128)S(1)}, f32[3,32,1,128]{3,2,1,0:T(1,128)S(1)}, u32[]{:S(2)}, u32[]{:S(2)}) collective-permute-start(f32[3,32,1,128]{3,2,1,0:T(1,128)S(1)} %slice.691), channel_id=1, source_target_pairs={{1,0},{2,1},{3,2},{5,4},{6,5},{7,6},{9,8},{10,9},{11,10},{13,12},{... | collective-permute-start | bytes 147464 | tf_op jit(solution)/shard_map/ppermute | solution.py:15
  54.4 5.6 %collective-permute-start.9 = (f32[3,1,8,128]{3,2,1,0:T(8,128)S(1)}, f32[3,1,8,128]{3,2,1,0:T(8,128)S(1)}, u32[]{:S(2)}, u32[]{:S(2)}) collective-permute-start(f32[3,1,8,128]{3,2,1,0:T(8,128)S(1)} %slice.697), channel_id=1, source_target_pairs={{4,0},{5,1},{6,2},{7,3},{12,8},{13,9},{14,10},{15,11},{20,16},{21,... | collective-permute-start | bytes 36872 | tf_op jit(solution)/shard_map/ppermute | solution.py:15
  60.4 7.6 %collective-permute-start.10 = (f32[3,32,1,128]{3,2,1,0:T(1,128)S(1)}, f32[3,32,1,128]{3,2,1,0:T(1,128)S(1)}, u32[]{:S(2)}, u32[]{:S(2)}) collective-permute-start(f32[3,32,1,128]{3,2,1,0:T(1,128)S(1)} %slice.701), channel_id=1, source_target_pairs={{0,1},{1,2},{2,3},{4,5},{5,6},{6,7},{8,9},{9,10},{10,11},{12,13},{... | collective-permute-start | bytes 147464 | tf_op jit(solution)/shard_map/ppermute | solution.py:15
  64.9 3.0 %collective-permute-start.11 = (f32[3,1,8,128]{3,2,1,0:T(8,128)S(1)}, f32[3,1,8,128]{3,2,1,0:T(8,128)S(1)}, u32[]{:S(2)}, u32[]{:S(2)}) collective-permute-start(f32[3,1,8,128]{3,2,1,0:T(8,128)S(1)} %slice.707), channel_id=1, source_target_pairs={{0,4},{1,5},{2,6},{3,7},{8,12},{9,13},{10,14},{11,15},{16,20},{17,... | collective-permute-start | bytes 36872 | tf_op jit(solution)/shard_map/ppermute | solution.py:15
  68.5 0.8 copy-start.4
  69.3 15.5 %copy-start.17 = (f32[3,32,8]{2,1,0:T(8,128)}, f32[3,32,8]{2,1,0:T(8,128)S(1)}, u32[]{:S(2)}) copy-start(f32[3,32,8]{2,1,0:T(8,128)S(1)} %get-tuple-element.46) | copy-start | bytes 9220
  69.3 15.5 %copy-start.20 = (f32[3,32,8]{2,1,0:T(8,128)}, f32[3,32,8]{2,1,0:T(8,128)S(1)}, u32[]{:S(2)}) copy-start(f32[3,32,8]{2,1,0:T(8,128)S(1)} %get-tuple-element.45) | copy-start | bytes 9220
  69.5 6.9 %collective-permute-start.16 = (f32[3,32,1,128]{3,2,1,0:T(1,128)S(1)}, f32[3,32,1,128]{3,2,1,0:T(1,128)S(1)}, u32[]{:S(2)}, u32[]{:S(2)}) collective-permute-start(f32[3,32,1,128]{3,2,1,0:T(1,128)S(1)} %slice.736), channel_id=1, source_target_pairs={{1,0},{2,1},{3,2},{5,4},{6,5},{7,6},{9,8},{10,9},{11,10},{13,12},{... | collective-permute-start | bytes 147464 | tf_op jit(solution)/shard_map/ppermute | solution.py:15
  70.8 5.6 %collective-permute-start.17 = (f32[3,1,8,128]{3,2,1,0:T(8,128)S(1)}, f32[3,1,8,128]{3,2,1,0:T(8,128)S(1)}, u32[]{:S(2)}, u32[]{:S(2)}) collective-permute-start(f32[3,1,8,128]{3,2,1,0:T(8,128)S(1)} %slice.742), channel_id=1, source_target_pairs={{4,0},{5,1},{6,2},{7,3},{12,8},{13,9},{14,10},{15,11},{20,16},{21,... | collective-permute-start | bytes 36872 | tf_op jit(solution)/shard_map/ppermute | solution.py:15
  76.7 7.7 %copy-start.6 = (f32[1,32,8,128]{3,2,1,0:T(8,128)}, f32[1,32,8,128]{3,2,1,0:T(8,128)S(1)}, u32[]{:S(2)}) copy-start(f32[1,32,8,128]{3,2,1,0:T(8,128)S(1)} %get-tuple-element.67) | copy-start | bytes 393220
  76.9 7.6 %collective-permute-start.18 = (f32[3,32,1,128]{3,2,1,0:T(1,128)S(1)}, f32[3,32,1,128]{3,2,1,0:T(1,128)S(1)}, u32[]{:S(2)}, u32[]{:S(2)}) collective-permute-start(f32[3,32,1,128]{3,2,1,0:T(1,128)S(1)} %slice.746), channel_id=1, source_target_pairs={{0,1},{1,2},{2,3},{4,5},{5,6},{6,7},{8,9},{9,10},{10,11},{12,13},{... | collective-permute-start | bytes 147464 | tf_op jit(solution)/shard_map/ppermute | solution.py:15
  81.4 3.0 %collective-permute-start.19 = (f32[3,1,8,128]{3,2,1,0:T(8,128)S(1)}, f32[3,1,8,128]{3,2,1,0:T(8,128)S(1)}, u32[]{:S(2)}, u32[]{:S(2)}) collective-permute-start(f32[3,1,8,128]{3,2,1,0:T(8,128)S(1)} %slice.752), channel_id=1, source_target_pairs={{0,4},{1,5},{2,6},{3,7},{8,12},{9,13},{10,14},{11,15},{16,20},{17,... | collective-permute-start | bytes 36872 | tf_op jit(solution)/shard_map/ppermute | solution.py:15
  84.8 0.7 copy-start.8
  84.8 0.7 copy-start.11
  84.8 0.7 copy-start.14
  86.1 7.0 %collective-permute-start.20 = (f32[3,32,1,128]{3,2,1,0:T(1,128)}, f32[3,32,1,128]{3,2,1,0:T(1,128)}, u32[]{:S(2)}, u32[]{:S(2)}) collective-permute-start(f32[3,32,1,128]{3,2,1,0:T(1,128)} %slice.758), channel_id=1, source_target_pairs={{1,0},{2,1},{3,2},{5,4},{6,5},{7,6},{9,8},{10,9},{11,10},{13,12},{... | collective-permute-start | bytes 147464 | tf_op jit(solution)/shard_map/ppermute | solution.py:15
  87.4 5.7 %collective-permute-start.21 = (f32[3,1,8,128]{3,2,1,0:T(8,128)S(1)}, f32[3,1,8,128]{3,2,1,0:T(8,128)}, u32[]{:S(2)}, u32[]{:S(2)}) collective-permute-start(f32[3,1,8,128]{3,2,1,0:T(8,128)S(1)} %slice.764), channel_id=1, source_target_pairs={{4,0},{5,1},{6,2},{7,3},{12,8},{13,9},{14,10},{15,11},{20,16},{21,... | collective-permute-start | bytes 36872 | tf_op jit(solution)/shard_map/ppermute | solution.py:15
  90.3 2.8 %copy-start.9 = (f32[1,32,8,128]{3,2,1,0:T(8,128)S(1)}, f32[1,32,8,128]{3,2,1,0:T(8,128)}, u32[]{:S(2)}) copy-start(f32[1,32,8,128]{3,2,1,0:T(8,128)} %copy-done.8) | copy-start | bytes 393220
  90.3 2.8 %copy-start.12 = (f32[1,32,8,128]{3,2,1,0:T(8,128)S(1)}, f32[1,32,8,128]{3,2,1,0:T(8,128)}, u32[]{:S(2)}) copy-start(f32[1,32,8,128]{3,2,1,0:T(8,128)} %copy-done.11) | copy-start | bytes 393220
  90.3 2.8 %copy-start.15 = (f32[1,32,8,128]{3,2,1,0:T(8,128)S(1)}, f32[1,32,8,128]{3,2,1,0:T(8,128)}, u32[]{:S(2)}) copy-start(f32[1,32,8,128]{3,2,1,0:T(8,128)} %copy-done.14) | copy-start | bytes 393220
  90.3 2.8 %copy-start.18 = (f32[3,32,8]{2,1,0:T(8,128)S(1)}, f32[3,32,8]{2,1,0:T(8,128)}, u32[]{:S(2)}) copy-start(f32[3,32,8]{2,1,0:T(8,128)} %copy-done.17) | copy-start | bytes 9220
  90.3 2.8 %copy-start.21 = (f32[3,32,8]{2,1,0:T(8,128)S(1)}, f32[3,32,8]{2,1,0:T(8,128)}, u32[]{:S(2)}) copy-start(f32[3,32,8]{2,1,0:T(8,128)} %copy-done.20) | copy-start | bytes 9220
  94.3 0.9 copy-start.7
  95.2 8.0 %copy-start.5 = (f32[3,32,8,128]{3,2,1,0:T(8,128)S(1)}, f32[3,32,8,128]{3,2,1,0:T(8,128)}, u32[]{:S(2)}) copy-start(f32[3,32,8,128]{3,2,1,0:T(8,128)} %copy-done.4) | copy-start | bytes 1179652
  95.4 9.2 %collective-permute-start.22 = (f32[3,32,1,128]{3,2,1,0:T(1,128)S(1)}, f32[3,32,1,128]{3,2,1,0:T(1,128)S(1)}, u32[]{:S(2)}, u32[]{:S(2)}) collective-permute-start(f32[3,32,1,128]{3,2,1,0:T(1,128)S(1)} %slice.768), channel_id=1, source_target_pairs={{0,1},{1,2},{2,3},{4,5},{5,6},{6,7},{8,9},{9,10},{10,11},{12,13},{... | collective-permute-start | bytes 147464 | tf_op jit(solution)/shard_map/ppermute | solution.py:15
  100.0 4.7 %collective-permute-start.23 = (f32[3,1,8,128]{3,2,1,0:T(8,128)S(1)}, f32[3,1,8,128]{3,2,1,0:T(8,128)S(1)}, u32[]{:S(2)}, u32[]{:S(2)}) collective-permute-start(f32[3,1,8,128]{3,2,1,0:T(8,128)S(1)} %slice.774), channel_id=1, source_target_pairs={{0,4},{1,5},{2,6},{3,7},{8,12},{9,13},{10,14},{11,15},{16,20},{17,... | collective-permute-start | bytes 36872 | tf_op jit(solution)/shard_map/ppermute | solution.py:15
  104.9 0.9 copy-start.23
  104.9 0.9 copy-start.25
  105.0 0.8 copy-start.28
  106.5 12.5 %copy-start.19 = (f32[3,32,8]{2,1,0:T(8,128)S(1)}, f32[3,32,8]{2,1,0:T(8,128)}, u32[]{:S(2)}) copy-start(f32[3,32,8]{2,1,0:T(8,128)} %copy-done.17) | copy-start | bytes 9220
  106.5 12.5 %copy-start.22 = (f32[3,32,8]{2,1,0:T(8,128)S(1)}, f32[3,32,8]{2,1,0:T(8,128)}, u32[]{:S(2)}) copy-start(f32[3,32,8]{2,1,0:T(8,128)} %copy-done.20) | copy-start | bytes 9220
  118.1 0.9 copy-start.13
  118.1 1.0 copy-start.16
  118.2 0.9 copy-start.10
where the time goes:
time: 121 us; the launch traced here: 120 us
  starting transfers between devices  58 us (48%)
  waiting for transfers between devices  19.5 us (16%)
  blocking collectives  17.8 us (15%)
  local copies, waits for them, and re-layouts  13.3 us (11%)
  other arithmetic  8.24 us (7%)
  between operations  3.44 us (3%)
    ppermute x24, starting transfers between devices, shifted_2(): return lax.ppermute(block, axis, route)  58 us
    ppermute x24, waiting for transfers between devices, shifted_2(): return lax.ppermute(block, axis, route)  19.5 us
    psum x1, blocking collectives, per_device(): summed = lax.psum(local_grad, 'wl')  11.6 us
    all_gather x1, blocking collectives, per_device(): tiles = lax.all_gather(design, 'wl', axis=0, tiled=True)  6.17 us
    unnamed x59, local copies, waits for them, and re-layouts  5.58 us
    slice x12, local copies, waits for them, and re-layouts, neighbours(): plane_y = stacked[:, :, :1] if upward else stacked[:, :, -1:]  3.04 us
  transfers between devices with their start and end apart: 24, of which 8 were waited for; matrix products, arithmetic and copies ran while one was open for 6% of the time, Pallas kernels for 0%

commit v1 on v0

--- a/solution.py
+++ b/solution.py
@@ -7,6 +7,11 @@
 Z0 = 64
 STEPS = 3
 time_step = 0.5
+
+
+def _reach_terms(patch, axis_tag):
+    current_block = jnp.sum(lax.all_gather(patch, axis_tag), axis=0)
+    return current_block
 
 
 def shifted_2(block, axis, distance):
@@ -108,7 +113,7 @@
         slab_depth,
     )
     local_grad = jnp.transpose(omega * omega * total, (2, 0, 1))
-    summed = lax.psum(local_grad, "wl")
+    summed = _reach_terms(local_grad, "wl")
     gradient = lax.dynamic_slice_in_dim(summed, lax.axis_index("wl") * owned, owned, 0)
     return (efield[None], adj_e[None], gradient)
 

time: 121 us -> 115 us (0.950)
  blocking collectives: 17.8 us -> 11.7 us
    psum x1 -> x0, blocking collectives: 11.6 us -> none  [per_device(): summed = lax.psum(local_grad, 'wl')]
    all_gather x0 -> x1, blocking collectives: none -> 5.55 us  [_reach_terms(): current_block = jnp.sum(lax.all_gather(patch, axis_tag), axis=0)]
    unnamed x59 -> x58, local copies, waits for them, and re-layouts: 5.58 us -> 4.93 us
where the time goes in v1:
time: 115 us; the launch traced here: 114 us
  starting transfers between devices  58 us (50%)
  waiting for transfers between devices  19.5 us (17%)
  local copies, waits for them, and re-layouts  13.3 us (12%)
  blocking collectives  11.7 us (10%)
  other arithmetic  8.26 us (7%)
  between operations  3.41 us (3%)
    ppermute x24, starting transfers between devices, shifted_2(): return lax.ppermute(block, axis, route)  58 us
    ppermute x24, waiting for transfers between devices, shifted_2(): return lax.ppermute(block, axis, route)  19.5 us
    all_gather x1, blocking collectives, per_device(): tiles = lax.all_gather(design, 'wl', axis=0, tiled=True)  6.17 us
    all_gather x1, blocking collectives, _reach_terms(): current_block = jnp.sum(lax.all_gather(patch, axis_tag), axis=0)  5.55 us
    unnamed x58, local copies, waits for them, and re-layouts  4.93 us
    slice x12, local copies, waits for them, and re-layouts, neighbours(): plane_y = stacked[:, :, :1] if upward else stacked[:, :, -1:]  3.04 us
  transfers between devices with their start and end apart: 24, of which 8 were waited for; matrix products, arithmetic and copies ran while one was open for 6% of the time, Pallas kernels for 0%

profile of v1, /device:TPU:0, one launch (start us, length us, event | category | flops | bytes accessed | tf_op | source)
XLA Modules:
  0.0 114.2 jit_solution(13119542429207054553)
XLA Ops:
  0.6 1.0 slice.645
  1.7 1.3 %collective-permute-start = (f32[3,32,1,128]{3,2,1,0:T(1,128)S(1)}, f32[3,32,1,128]{3,2,1,0:T(1,128)S(1)}, u32[]{:S(2)}, u32[]{:S(2)}) collective-permute-start(f32[3,32,1,128]{3,2,1,0:T(1,128)S(1)} %slice.645), channel_id=1, source_target_pairs={{1,0},{2,1},{3,2},{5,4},{6,5},{7,6},{9,8},{10,9},{11,10},{13,12},{... | collective-permute-start | bytes 147464 | tf_op jit(solution)/shard_map/ppermute | solution.py:20
  3.0 0.7 slice.651
  3.7 1.3 %collective-permute-start.1 = (f32[3,1,8,128]{3,2,1,0:T(8,128)S(1)}, f32[3,1,8,128]{3,2,1,0:T(8,128)S(1)}, u32[]{:S(2)}, u32[]{:S(2)}) collective-permute-start(f32[3,1,8,128]{3,2,1,0:T(8,128)S(1)} %slice.651), channel_id=1, source_target_pairs={{4,0},{5,1},{6,2},{7,3},{12,8},{13,9},{14,10},{15,11},{20,16},{21,... | collective-permute-start | bytes 36872 | tf_op jit(solution)/shard_map/ppermute | solution.py:20
  5.0 1.0 slice.714
  6.0 1.4 %collective-permute-start.12 = (f32[3,32,1,128]{3,2,1,0:T(1,128)S(1)}, f32[3,32,1,128]{3,2,1,0:T(1,128)S(1)}, u32[]{:S(2)}, u32[]{:S(2)}) collective-permute-start(f32[3,32,1,128]{3,2,1,0:T(1,128)S(1)} %slice.714), channel_id=1, source_target_pairs={{1,0},{2,1},{3,2},{5,4},{6,5},{7,6},{9,8},{10,9},{11,10},{13,12},{... | collective-permute-start | bytes 147464 | tf_op jit(solution)/shard_map/ppermute | solution.py:20
  7.4 0.7 slice.720
  8.2 1.3 %collective-permute-start.13 = (f32[3,1,8,128]{3,2,1,0:T(8,128)S(1)}, f32[3,1,8,128]{3,2,1,0:T(8,128)S(1)}, u32[]{:S(2)}, u32[]{:S(2)}) collective-permute-start(f32[3,1,8,128]{3,2,1,0:T(8,128)S(1)} %slice.720), channel_id=1, source_target_pairs={{4,0},{5,1},{6,2},{7,3},{12,8},{13,9},{14,10},{15,11},{20,16},{21,... | collective-permute-start | bytes 36872 | tf_op jit(solution)/shard_map/ppermute | solution.py:20
  9.5 6.2 %all_gather.9 = f32[8,32,8]{1,2,0:T(8,128)S(1)} all-gather(f32[2,32,8]{1,2,0:T(8,128)S(1)} %copy-done.26), channel_id=1, replica_groups=mesh['wl'=4,'gx'=2,'gy'=4] {'wl'}, dimensions={0}, use_global_device_ids=true | all-gather | bytes 10240 | tf_op jit(solution)/shard_map/all_gather | solution.py:88
  17.6 1.0 copy-done
  19.1 0.6 copy-done.27
  20.1 0.9 copy-done.1
  21.1 5.2 %collective-permute-start.2 = (f32[3,32,1,128]{3,2,1,0:T(1,128)S(1)}, f32[3,32,1,128]{3,2,1,0:T(1,128)S(1)}, u32[]{:S(2)}, u32[]{:S(2)}) collective-permute-start(f32[3,32,1,128]{3,2,1,0:T(1,128)S(1)} %slice.655), channel_id=1, source_target_pairs={{0,1},{1,2},{2,3},{4,5},{5,6},{6,7},{8,9},{9,10},{10,11},{12,13},{... | collective-permute-start | bytes 147464 | tf_op jit(solution)/shard_map/ppermute | solution.py:20
  26.3 4.5 %collective-permute-start.3 = (f32[3,1,8,128]{3,2,1,0:T(8,128)S(1)}, f32[3,1,8,128]{3,2,1,0:T(8,128)S(1)}, u32[]{:S(2)}, u32[]{:S(2)}) collective-permute-start(f32[3,1,8,128]{3,2,1,0:T(8,128)S(1)} %slice.661), channel_id=1, source_target_pairs={{0,4},{1,5},{2,6},{3,7},{8,12},{9,13},{10,14},{11,15},{16,20},{17,... | collective-permute-start | bytes 36872 | tf_op jit(solution)/shard_map/ppermute | solution.py:20
  31.1 1.2 %collective-permute-done.3 = f32[3,1,8,128]{3,2,1,0:T(8,128)S(1)} collective-permute-done((f32[3,1,8,128]{3,2,1,0:T(8,128)S(1)}, f32[3,1,8,128]{3,2,1,0:T(8,128)S(1)}, u32[]{:S(2)}, u32[]{:S(2)}) %collective-permute-start.3) | collective-permute-done | bytes 12320 | tf_op jit(solution)/shard_map/ppermute | solution.py:20
  32.3 0.2 pad_subtract_fusion.10
  32.7 1.3 %collective-permute-start.4 = (f32[3,32,1,128]{3,2,1,0:T(1,128)S(1)}, f32[3,32,1,128]{3,2,1,0:T(1,128)S(1)}, u32[]{:S(2)}, u32[]{:S(2)}) collective-permute-start(f32[3,32,1,128]{3,2,1,0:T(1,128)S(1)} %slice.668), channel_id=1, source_target_pairs={{1,0},{2,1},{3,2},{5,4},{6,5},{7,6},{9,8},{10,9},{11,10},{13,12},{... | collective-permute-start | bytes 147464 | tf_op jit(solution)/shard_map/ppermute | solution.py:20
  34.0 1.3 %collective-permute-start.5 = (f32[3,1,8,128]{3,2,1,0:T(8,128)S(1)}, f32[3,1,8,128]{3,2,1,0:T(8,128)S(1)}, u32[]{:S(2)}, u32[]{:S(2)}) collective-permute-start(f32[3,1,8,128]{3,2,1,0:T(8,128)S(1)} %slice.674), channel_id=1, source_target_pairs={{4,0},{5,1},{6,2},{7,3},{12,8},{13,9},{14,10},{15,11},{20,16},{21,... | collective-permute-start | bytes 36872 | tf_op jit(solution)/shard_map/ppermute | solution.py:20
  35.4 0.2 slice.670
  35.6 4.0 %collective-permute-done.5 = f32[3,1,8,128]{3,2,1,0:T(8,128)S(1)} collective-permute-done((f32[3,1,8,128]{3,2,1,0:T(8,128)S(1)}, f32[3,1,8,128]{3,2,1,0:T(8,128)S(1)}, u32[]{:S(2)}, u32[]{:S(2)}) %collective-permute-start.5) | collective-permute-done | bytes 12320 | tf_op jit(solution)/shard_map/ppermute | solution.py:20
  40.0 4.6 %collective-permute-start.6 = (f32[3,32,1,128]{3,2,1,0:T(1,128)S(1)}, f32[3,32,1,128]{3,2,1,0:T(1,128)S(1)}, u32[]{:S(2)}, u32[]{:S(2)}) collective-permute-start(f32[3,32,1,128]{3,2,1,0:T(1,128)S(1)} %slice.678), channel_id=1, source_target_pairs={{0,1},{1,2},{2,3},{4,5},{5,6},{6,7},{8,9},{9,10},{10,11},{12,13},{... | collective-permute-start | bytes 147464 | tf_op jit(solution)/shard_map/ppermute | solution.py:20
  44.5 2.7 %collective-permute-start.7 = (f32[3,1,8,128]{3,2,1,0:T(8,128)S(1)}, f32[3,1,8,128]{3,2,1,0:T(8,128)S(1)}, u32[]{:S(2)}, u32[]{:S(2)}) collective-permute-start(f32[3,1,8,128]{3,2,1,0:T(8,128)S(1)} %slice.684), channel_id=1, source_target_pairs={{0,4},{1,5},{2,6},{3,7},{8,12},{9,13},{10,14},{11,15},{16,20},{17,... | collective-permute-start | bytes 36872 | tf_op jit(solution)/shard_map/ppermute | solution.py:20
  47.4 3.9 %collective-permute-start.14 = (f32[3,32,1,128]{3,2,1,0:T(1,128)S(1)}, f32[3,32,1,128]{3,2,1,0:T(1,128)S(1)}, u32[]{:S(2)}, u32[]{:S(2)}) collective-permute-start(f32[3,32,1,128]{3,2,1,0:T(1,128)S(1)} %slice.724), channel_id=1, source_target_pairs={{0,1},{1,2},{2,3},{4,5},{5,6},{6,7},{8,9},{9,10},{10,11},{12,13},{... | collective-permute-start | bytes 147464 | tf_op jit(solution)/shard_map/ppermute | solution.py:20
  51.3 1.3 %collective-permute-start.15 = (f32[3,1,8,128]{3,2,1,0:T(8,128)S(1)}, f32[3,1,8,128]{3,2,1,0:T(8,128)S(1)}, u32[]{:S(2)}, u32[]{:S(2)}) collective-permute-start(f32[3,1,8,128]{3,2,1,0:T(8,128)S(1)} %slice.730), channel_id=1, source_target_pairs={{0,4},{1,5},{2,6},{3,7},{8,12},{9,13},{10,14},{11,15},{16,20},{17,... | collective-permute-start | bytes 36872 | tf_op jit(solution)/shard_map/ppermute | solution.py:20
  52.6 0.2 pad_subtract_fusion.8
  53.1 1.3 %collective-permute-start.8 = (f32[3,32,1,128]{3,2,1,0:T(1,128)S(1)}, f32[3,32,1,128]{3,2,1,0:T(1,128)S(1)}, u32[]{:S(2)}, u32[]{:S(2)}) collective-permute-start(f32[3,32,1,128]{3,2,1,0:T(1,128)S(1)} %slice.691), channel_id=1, source_target_pairs={{1,0},{2,1},{3,2},{5,4},{6,5},{7,6},{9,8},{10,9},{11,10},{13,12},{... | collective-permute-start | bytes 147464 | tf_op jit(solution)/shard_map/ppermute | solution.py:20
  54.4 1.3 %collective-permute-start.9 = (f32[3,1,8,128]{3,2,1,0:T(8,128)S(1)}, f32[3,1,8,128]{3,2,1,0:T(8,128)S(1)}, u32[]{:S(2)}, u32[]{:S(2)}) collective-permute-start(f32[3,1,8,128]{3,2,1,0:T(8,128)S(1)} %slice.697), channel_id=1, source_target_pairs={{4,0},{5,1},{6,2},{7,3},{12,8},{13,9},{14,10},{15,11},{20,16},{21,... | collective-permute-start | bytes 36872 | tf_op jit(solution)/shard_map/ppermute | solution.py:20
  55.8 0.2 pad_subtract_fusion.4
  56.2 3.8 %collective-permute-done.9 = f32[3,1,8,128]{3,2,1,0:T(8,128)S(1)} collective-permute-done((f32[3,1,8,128]{3,2,1,0:T(8,128)S(1)}, f32[3,1,8,128]{3,2,1,0:T(8,128)S(1)}, u32[]{:S(2)}, u32[]{:S(2)}) %collective-permute-start.9) | collective-permute-done | bytes 12320 | tf_op jit(solution)/shard_map/ppermute | solution.py:20
  60.4 4.5 %collective-permute-start.10 = (f32[3,32,1,128]{3,2,1,0:T(1,128)S(1)}, f32[3,32,1,128]{3,2,1,0:T(1,128)S(1)}, u32[]{:S(2)}, u32[]{:S(2)}) collective-permute-start(f32[3,32,1,128]{3,2,1,0:T(1,128)S(1)} %slice.701), channel_id=1, source_target_pairs={{0,1},{1,2},{2,3},{4,5},{5,6},{6,7},{8,9},{9,10},{10,11},{12,13},{... | collective-permute-start | bytes 147464 | tf_op jit(solution)/shard_map/ppermute | solution.py:20
  64.9 1.6 %collective-permute-start.11 = (f32[3,1,8,128]{3,2,1,0:T(8,128)S(1)}, f32[3,1,8,128]{3,2,1,0:T(8,128)S(1)}, u32[]{:S(2)}, u32[]{:S(2)}) collective-permute-start(f32[3,1,8,128]{3,2,1,0:T(8,128)S(1)} %slice.707), channel_id=1, source_target_pairs={{0,4},{1,5},{2,6},{3,7},{8,12},{9,13},{10,14},{11,15},{16,20},{17,... | collective-permute-start | bytes 36872 | tf_op jit(solution)/shard_map/ppermute | solution.py:20
  66.7 1.3 %collective-permute-done.11 = f32[3,1,8,128]{3,2,1,0:T(8,128)S(1)} collective-permute-done((f32[3,1,8,128]{3,2,1,0:T(8,128)S(1)}, f32[3,1,8,128]{3,2,1,0:T(8,128)S(1)}, u32[]{:S(2)}, u32[]{:S(2)}) %collective-permute-start.11) | collective-permute-done | bytes 12320 | tf_op jit(solution)/shard_map/ppermute | solution.py:20
  68.0 0.3 pad_subtract_fusion.6
  68.5 0.8 multiply_reduce_fusion
  69.3 0.2 fusion.21
  69.5 1.3 %collective-permute-start.16 = (f32[3,32,1,128]{3,2,1,0:T(1,128)S(1)}, f32[3,32,1,128]{3,2,1,0:T(1,128)S(1)}, u32[]{:S(2)}, u32[]{:S(2)}) collective-permute-start(f32[3,32,1,128]{3,2,1,0:T(1,128)S(1)} %slice.736), channel_id=1, source_target_pairs={{1,0},{2,1},{3,2},{5,4},{6,5},{7,6},{9,8},{10,9},{11,10},{13,12},{... | collective-permute-start | bytes 147464 | tf_op jit(solution)/shard_map/ppermute | solution.py:20
  70.8 1.3 %collective-permute-start.17 = (f32[3,1,8,128]{3,2,1,0:T(8,128)S(1)}, f32[3,1,8,128]{3,2,1,0:T(8,128)S(1)}, u32[]{:S(2)}, u32[]{:S(2)}) collective-permute-start(f32[3,1,8,128]{3,2,1,0:T(8,128)S(1)} %slice.742), channel_id=1, source_target_pairs={{4,0},{5,1},{6,2},{7,3},{12,8},{13,9},{14,10},{15,11},{20,16},{21,... | collective-permute-start | bytes 36872 | tf_op jit(solution)/shard_map/ppermute | solution.py:20
  72.4 4.0 %collective-permute-done.17 = f32[3,1,8,128]{3,2,1,0:T(8,128)S(1)} collective-permute-done((f32[3,1,8,128]{3,2,1,0:T(8,128)S(1)}, f32[3,1,8,128]{3,2,1,0:T(8,128)S(1)}, u32[]{:S(2)}, u32[]{:S(2)}) %collective-permute-start.17) | collective-permute-done | bytes 12320 | tf_op jit(solution)/shard_map/ppermute | solution.py:20
  76.4 0.2 pad_subtract_fusion.3
  76.9 4.5 %collective-permute-start.18 = (f32[3,32,1,128]{3,2,1,0:T(1,128)S(1)}, f32[3,32,1,128]{3,2,1,0:T(1,128)S(1)}, u32[]{:S(2)}, u32[]{:S(2)}) collective-permute-start(f32[3,32,1,128]{3,2,1,0:T(1,128)S(1)} %slice.746), channel_id=1, source_target_pairs={{0,1},{1,2},{2,3},{4,5},{5,6},{6,7},{8,9},{9,10},{10,11},{12,13},{... | collective-permute-start | bytes 147464 | tf_op jit(solution)/shard_map/ppermute | solution.py:20
  81.4 1.6 %collective-permute-start.19 = (f32[3,1,8,128]{3,2,1,0:T(8,128)S(1)}, f32[3,1,8,128]{3,2,1,0:T(8,128)S(1)}, u32[]{:S(2)}, u32[]{:S(2)}) collective-permute-start(f32[3,1,8,128]{3,2,1,0:T(8,128)S(1)} %slice.752), channel_id=1, source_target_pairs={{0,4},{1,5},{2,6},{3,7},{8,12},{9,13},{10,14},{11,15},{16,20},{17,... | collective-permute-start | bytes 36872 | tf_op jit(solution)/shard_map/ppermute | solution.py:20
  83.1 1.4 %collective-permute-done.19 = f32[3,1,8,128]{3,2,1,0:T(8,128)S(1)} collective-permute-done((f32[3,1,8,128]{3,2,1,0:T(8,128)S(1)}, f32[3,1,8,128]{3,2,1,0:T(8,128)S(1)}, u32[]{:S(2)}, u32[]{:S(2)}) %collective-permute-start.19) | collective-permute-done | bytes 12320 | tf_op jit(solution)/shard_map/ppermute | solution.py:20
  84.5 0.2 pad_subtract_fusion.2
  84.8 0.3 fusion.24
  85.1 0.3 copy-done.8
  85.5 0.6 slice.758
  86.1 1.3 %collective-permute-start.20 = (f32[3,32,1,128]{3,2,1,0:T(1,128)}, f32[3,32,1,128]{3,2,1,0:T(1,128)}, u32[]{:S(2)}, u32[]{:S(2)}) collective-permute-start(f32[3,32,1,128]{3,2,1,0:T(1,128)} %slice.758), channel_id=1, source_target_pairs={{1,0},{2,1},{3,2},{5,4},{6,5},{7,6},{9,8},{10,9},{11,10},{13,12},{... | collective-permute-start | bytes 147464 | tf_op jit(solution)/shard_map/ppermute | solution.py:20
  87.4 1.3 %collective-permute-start.21 = (f32[3,1,8,128]{3,2,1,0:T(8,128)S(1)}, f32[3,1,8,128]{3,2,1,0:T(8,128)}, u32[]{:S(2)}, u32[]{:S(2)}) collective-permute-start(f32[3,1,8,128]{3,2,1,0:T(8,128)S(1)} %slice.764), channel_id=1, source_target_pairs={{4,0},{5,1},{6,2},{7,3},{12,8},{13,9},{14,10},{15,11},{20,16},{21,... | collective-permute-start | bytes 36872 | tf_op jit(solution)/shard_map/ppermute | solution.py:20
  88.7 0.8 slice.784
  89.5 0.6 slice.786
  90.4 2.8 %collective-permute-done.21 = f32[3,1,8,128]{3,2,1,0:T(8,128)} collective-permute-done((f32[3,1,8,128]{3,2,1,0:T(8,128)S(1)}, f32[3,1,8,128]{3,2,1,0:T(8,128)}, u32[]{:S(2)}, u32[]{:S(2)}) %collective-permute-start.21) | collective-permute-done | bytes 12320 | tf_op jit(solution)/shard_map/ppermute | solution.py:20
  93.2 1.2 %pad_subtract_fusion.1 = (f32[3,32,8,128]{3,2,1,0:T(8,128)S(1)}, f32[3,32,8,128]{3,2,1,0:T(8,128)S(1)}, f32[3,32,8,128]{3,2,1,0:T(8,128)S(1)}) fusion(f32[3,32,8,127]{3,2,1,0:T(8,128)S(1)} %slice.760, f32[3,1,8,128]{3,2,1,0:T(8,128)} %collective-permute-done.21, f32[3,31,8,128]{3,2,1,0:T(8,128)S(1)} %slice.763, ...), kind=kLoop, calls=%fused_computation.70 | loop fusion | flops 1671168 | bytes 3673600 | tf_op jit(solution)/shard_map/sub | solution.py:36
  94.4 0.8 copy-done.7
  95.4 4.5 %collective-permute-start.22 = (f32[3,32,1,128]{3,2,1,0:T(1,128)S(1)}, f32[3,32,1,128]{3,2,1,0:T(1,128)S(1)}, u32[]{:S(2)}, u32[]{:S(2)}) collective-permute-start(f32[3,32,1,128]{3,2,1,0:T(1,128)S(1)} %slice.768), channel_id=1, source_target_pairs={{0,1},{1,2},{2,3},{4,5},{5,6},{6,7},{8,9},{9,10},{10,11},{12,13},{... | collective-permute-start | bytes 147464 | tf_op jit(solution)/shard_map/ppermute | solution.py:20
  100.0 3.3 %collective-permute-start.23 = (f32[3,1,8,128]{3,2,1,0:T(8,128)S(1)}, f32[3,1,8,128]{3,2,1,0:T(8,128)S(1)}, u32[]{:S(2)}, u32[]{:S(2)}) collective-permute-start(f32[3,1,8,128]{3,2,1,0:T(8,128)S(1)} %slice.774), channel_id=1, source_target_pairs={{0,4},{1,5},{2,6},{3,7},{8,12},{9,13},{10,14},{11,15},{16,20},{17,... | collective-permute-start | bytes 36872 | tf_op jit(solution)/shard_map/ppermute | solution.py:20
  103.3 0.3 fusion.6
  103.6 1.1 collective-permute-done.23
  104.7 0.3 pad_subtract_fusion
  105.0 0.8 copy-done.23
  105.8 0.6 fusion.5
  106.6 5.6 %all-gather = f32[32,32,8]{1,2,0:T(8,128)S(1)} all-gather(f32[8,32,8]{1,2,0:T(8,128)S(1)} %copy.18), channel_id=2, replica_groups=mesh['wl'=4,'gx'=2,'gy'=4] {'wl'}, dimensions={0}, use_global_device_ids=true | all-gather | bytes 40960 | tf_op jit(solution)/shard_map/all_gather | solution.py:13
  112.2 0.6 constant_dynamic-slice_fusion
  112.8 0.3 copy-done.10
  113.1 1.1 fusion.19
  (146 shorter events, 4.6 us)
Async XLA Ops:
  1.7 18.2 %collective-permute-start = (f32[3,32,1,128]{3,2,1,0:T(1,128)S(1)}, f32[3,32,1,128]{3,2,1,0:T(1,128)S(1)}, u32[]{:S(2)}, u32[]{:S(2)}) collective-permute-start(f32[3,32,1,128]{3,2,1,0:T(1,128)S(1)} %slice.645), channel_id=1, source_target_pairs={{1,0},{2,1},{3,2},{5,4},{6,5},{7,6},{9,8},{10,9},{11,10},{13,12},{... | collective-permute-start | bytes 147464 | tf_op jit(solution)/shard_map/ppermute | solution.py:20
  3.7 16.2 %collective-permute-start.1 = (f32[3,1,8,128]{3,2,1,0:T(8,128)S(1)}, f32[3,1,8,128]{3,2,1,0:T(8,128)S(1)}, u32[]{:S(2)}, u32[]{:S(2)}) collective-permute-start(f32[3,1,8,128]{3,2,1,0:T(8,128)S(1)} %slice.651), channel_id=1, source_target_pairs={{4,0},{5,1},{6,2},{7,3},{12,8},{13,9},{14,10},{15,11},{20,16},{21,... | collective-permute-start | bytes 36872 | tf_op jit(solution)/shard_map/ppermute | solution.py:20
  5.0 4.5 %copy-start.26 = (f32[2,32,8]{1,2,0:T(8,128)S(1)}, f32[2,32,8]{1,2,0:T(8,128)}, u32[]{:S(2)}) copy-start(f32[2,32,8]{1,2,0:T(8,128)} %param.20) | copy-start | bytes 6148
  6.0 9.8 %copy-start.24 = (f32[32,8,128]{2,1,0:T(8,128)S(1)}, f32[32,8,128]{2,1,0:T(8,128)}, u32[]{:S(2)}) copy-start(f32[32,8,128]{2,1,0:T(8,128)} %param.19) | copy-start | bytes 393220
  6.0 24.9 %collective-permute-start.12 = (f32[3,32,1,128]{3,2,1,0:T(1,128)S(1)}, f32[3,32,1,128]{3,2,1,0:T(1,128)S(1)}, u32[]{:S(2)}, u32[]{:S(2)}) collective-permute-start(f32[3,32,1,128]{3,2,1,0:T(1,128)S(1)} %slice.714), channel_id=1, source_target_pairs={{1,0},{2,1},{3,2},{5,4},{6,5},{7,6},{9,8},{10,9},{11,10},{13,12},{... | collective-permute-start | bytes 147464 | tf_op jit(solution)/shard_map/ppermute | solution.py:20
  8.2 22.7 %collective-permute-start.13 = (f32[3,1,8,128]{3,2,1,0:T(8,128)S(1)}, f32[3,1,8,128]{3,2,1,0:T(8,128)S(1)}, u32[]{:S(2)}, u32[]{:S(2)}) collective-permute-start(f32[3,1,8,128]{3,2,1,0:T(8,128)S(1)} %slice.720), channel_id=1, source_target_pairs={{4,0},{5,1},{6,2},{7,3},{12,8},{13,9},{14,10},{15,11},{20,16},{21,... | collective-permute-start | bytes 36872 | tf_op jit(solution)/shard_map/ppermute | solution.py:20
  15.8 1.6 %copy-start.3 = (f32[1,3,32,8,128]{4,3,2,1,0:T(8,128)S(1)}, f32[1,3,32,8,128]{4,3,2,1,0:T(8,128)}, u32[]{:S(2)}) copy-start(f32[1,3,32,8,128]{4,3,2,1,0:T(8,128)} %param.15) | copy-start | bytes 1179652
  17.6 1.0 copy-start
  19.0 0.7 copy-start.27
  20.0 1.0 copy-start.1
  21.1 11.2 %collective-permute-start.2 = (f32[3,32,1,128]{3,2,1,0:T(1,128)S(1)}, f32[3,32,1,128]{3,2,1,0:T(1,128)S(1)}, u32[]{:S(2)}, u32[]{:S(2)}) collective-permute-start(f32[3,32,1,128]{3,2,1,0:T(1,128)S(1)} %slice.655), channel_id=1, source_target_pairs={{0,1},{1,2},{2,3},{4,5},{5,6},{6,7},{8,9},{9,10},{10,11},{12,13},{... | collective-permute-start | bytes 147464 | tf_op jit(solution)/shard_map/ppermute | solution.py:20
  26.3 5.9 %collective-permute-start.3 = (f32[3,1,8,128]{3,2,1,0:T(8,128)S(1)}, f32[3,1,8,128]{3,2,1,0:T(8,128)S(1)}, u32[]{:S(2)}, u32[]{:S(2)}) collective-permute-start(f32[3,1,8,128]{3,2,1,0:T(8,128)S(1)} %slice.661), channel_id=1, source_target_pairs={{0,4},{1,5},{2,6},{3,7},{8,12},{9,13},{10,14},{11,15},{16,20},{17,... | collective-permute-start | bytes 36872 | tf_op jit(solution)/shard_map/ppermute | solution.py:20
  32.7 6.9 %collective-permute-start.4 = (f32[3,32,1,128]{3,2,1,0:T(1,128)S(1)}, f32[3,32,1,128]{3,2,1,0:T(1,128)S(1)}, u32[]{:S(2)}, u32[]{:S(2)}) collective-permute-start(f32[3,32,1,128]{3,2,1,0:T(1,128)S(1)} %slice.668), channel_id=1, source_target_pairs={{1,0},{2,1},{3,2},{5,4},{6,5},{7,6},{9,8},{10,9},{11,10},{13,12},{... | collective-permute-start | bytes 147464 | tf_op jit(solution)/shard_map/ppermute | solution.py:20
  34.0 5.6 %collective-permute-start.5 = (f32[3,1,8,128]{3,2,1,0:T(8,128)S(1)}, f32[3,1,8,128]{3,2,1,0:T(8,128)S(1)}, u32[]{:S(2)}, u32[]{:S(2)}) collective-permute-start(f32[3,1,8,128]{3,2,1,0:T(8,128)S(1)} %slice.674), channel_id=1, source_target_pairs={{4,0},{5,1},{6,2},{7,3},{12,8},{13,9},{14,10},{15,11},{20,16},{21,... | collective-permute-start | bytes 36872 | tf_op jit(solution)/shard_map/ppermute | solution.py:20
  39.8 7.4 %copy-start.2 = (f32[1,3,32,8,128]{4,3,2,1,0:T(8,128)S(1)}, f32[1,3,32,8,128]{4,3,2,1,0:T(8,128)}, u32[]{:S(2)}) copy-start(f32[1,3,32,8,128]{4,3,2,1,0:T(8,128)} %param.18) | copy-start | bytes 1179652
  40.0 12.7 %collective-permute-start.6 = (f32[3,32,1,128]{3,2,1,0:T(1,128)S(1)}, f32[3,32,1,128]{3,2,1,0:T(1,128)S(1)}, u32[]{:S(2)}, u32[]{:S(2)}) collective-permute-start(f32[3,32,1,128]{3,2,1,0:T(1,128)S(1)} %slice.678), channel_id=1, source_target_pairs={{0,1},{1,2},{2,3},{4,5},{5,6},{6,7},{8,9},{9,10},{10,11},{12,13},{... | collective-permute-start | bytes 147464 | tf_op jit(solution)/shard_map/ppermute | solution.py:20
  44.5 8.1 %collective-permute-start.7 = (f32[3,1,8,128]{3,2,1,0:T(8,128)S(1)}, f32[3,1,8,128]{3,2,1,0:T(8,128)S(1)}, u32[]{:S(2)}, u32[]{:S(2)}) collective-permute-start(f32[3,1,8,128]{3,2,1,0:T(8,128)S(1)} %slice.684), channel_id=1, source_target_pairs={{0,4},{1,5},{2,6},{3,7},{8,12},{9,13},{10,14},{11,15},{16,20},{17,... | collective-permute-start | bytes 36872 | tf_op jit(solution)/shard_map/ppermute | solution.py:20
  47.4 8.4 %collective-permute-start.14 = (f32[3,32,1,128]{3,2,1,0:T(1,128)S(1)}, f32[3,32,1,128]{3,2,1,0:T(1,128)S(1)}, u32[]{:S(2)}, u32[]{:S(2)}) collective-permute-start(f32[3,32,1,128]{3,2,1,0:T(1,128)S(1)} %slice.724), channel_id=1, source_target_pairs={{0,1},{1,2},{2,3},{4,5},{5,6},{6,7},{8,9},{9,10},{10,11},{12,13},{... | collective-permute-start | bytes 147464 | tf_op jit(solution)/shard_map/ppermute | solution.py:20
  51.3 4.5 %collective-permute-start.15 = (f32[3,1,8,128]{3,2,1,0:T(8,128)S(1)}, f32[3,1,8,128]{3,2,1,0:T(8,128)S(1)}, u32[]{:S(2)}, u32[]{:S(2)}) collective-permute-start(f32[3,1,8,128]{3,2,1,0:T(8,128)S(1)} %slice.730), channel_id=1, source_target_pairs={{0,4},{1,5},{2,6},{3,7},{8,12},{9,13},{10,14},{11,15},{16,20},{17,... | collective-permute-start | bytes 36872 | tf_op jit(solution)/shard_map/ppermute | solution.py:20
  53.1 6.9 %collective-permute-start.8 = (f32[3,32,1,128]{3,2,1,0:T(1,128)S(1)}, f32[3,32,1,128]{3,2,1,0:T(1,128)S(1)}, u32[]{:S(2)}, u32[]{:S(2)}) collective-permute-start(f32[3,32,1,128]{3,2,1,0:T(1,128)S(1)} %slice.691), channel_id=1, source_target_pairs={{1,0},{2,1},{3,2},{5,4},{6,5},{7,6},{9,8},{10,9},{11,10},{13,12},{... | collective-permute-start | bytes 147464 | tf_op jit(solution)/shard_map/ppermute | solution.py:20
  54.4 5.6 %collective-permute-start.9 = (f32[3,1,8,128]{3,2,1,0:T(8,128)S(1)}, f32[3,1,8,128]{3,2,1,0:T(8,128)S(1)}, u32[]{:S(2)}, u32[]{:S(2)}) collective-permute-start(f32[3,1,8,128]{3,2,1,0:T(8,128)S(1)} %slice.697), channel_id=1, source_target_pairs={{4,0},{5,1},{6,2},{7,3},{12,8},{13,9},{14,10},{15,11},{20,16},{21,... | collective-permute-start | bytes 36872 | tf_op jit(solution)/shard_map/ppermute | solution.py:20
  60.4 7.6 %collective-permute-start.10 = (f32[3,32,1,128]{3,2,1,0:T(1,128)S(1)}, f32[3,32,1,128]{3,2,1,0:T(1,128)S(1)}, u32[]{:S(2)}, u32[]{:S(2)}) collective-permute-start(f32[3,32,1,128]{3,2,1,0:T(1,128)S(1)} %slice.701), channel_id=1, source_target_pairs={{0,1},{1,2},{2,3},{4,5},{5,6},{6,7},{8,9},{9,10},{10,11},{12,13},{... | collective-permute-start | bytes 147464 | tf_op jit(solution)/shard_map/ppermute | solution.py:20
  64.9 3.0 %collective-permute-start.11 = (f32[3,1,8,128]{3,2,1,0:T(8,128)S(1)}, f32[3,1,8,128]{3,2,1,0:T(8,128)S(1)}, u32[]{:S(2)}, u32[]{:S(2)}) collective-permute-start(f32[3,1,8,128]{3,2,1,0:T(8,128)S(1)} %slice.707), channel_id=1, source_target_pairs={{0,4},{1,5},{2,6},{3,7},{8,12},{9,13},{10,14},{11,15},{16,20},{17,... | collective-permute-start | bytes 36872 | tf_op jit(solution)/shard_map/ppermute | solution.py:20
  68.5 0.8 copy-start.4
  69.3 15.5 %copy-start.17 = (f32[3,32,8]{2,1,0:T(8,128)}, f32[3,32,8]{2,1,0:T(8,128)S(1)}, u32[]{:S(2)}) copy-start(f32[3,32,8]{2,1,0:T(8,128)S(1)} %get-tuple-element.43) | copy-start | bytes 9220
  69.3 15.5 %copy-start.20 = (f32[3,32,8]{2,1,0:T(8,128)}, f32[3,32,8]{2,1,0:T(8,128)S(1)}, u32[]{:S(2)}) copy-start(f32[3,32,8]{2,1,0:T(8,128)S(1)} %get-tuple-element.42) | copy-start | bytes 9220
  69.5 6.9 %collective-permute-start.16 = (f32[3,32,1,128]{3,2,1,0:T(1,128)S(1)}, f32[3,32,1,128]{3,2,1,0:T(1,128)S(1)}, u32[]{:S(2)}, u32[]{:S(2)}) collective-permute-start(f32[3,32,1,128]{3,2,1,0:T(1,128)S(1)} %slice.736), channel_id=1, source_target_pairs={{1,0},{2,1},{3,2},{5,4},{6,5},{7,6},{9,8},{10,9},{11,10},{13,12},{... | collective-permute-start | bytes 147464 | tf_op jit(solution)/shard_map/ppermute | solution.py:20
  70.8 5.6 %collective-permute-start.17 = (f32[3,1,8,128]{3,2,1,0:T(8,128)S(1)}, f32[3,1,8,128]{3,2,1,0:T(8,128)S(1)}, u32[]{:S(2)}, u32[]{:S(2)}) collective-permute-start(f32[3,1,8,128]{3,2,1,0:T(8,128)S(1)} %slice.742), channel_id=1, source_target_pairs={{4,0},{5,1},{6,2},{7,3},{12,8},{13,9},{14,10},{15,11},{20,16},{21,... | collective-permute-start | bytes 36872 | tf_op jit(solution)/shard_map/ppermute | solution.py:20
  76.7 7.7 %copy-start.6 = (f32[1,32,8,128]{3,2,1,0:T(8,128)}, f32[1,32,8,128]{3,2,1,0:T(8,128)S(1)}, u32[]{:S(2)}) copy-start(f32[1,32,8,128]{3,2,1,0:T(8,128)S(1)} %get-tuple-element.64) | copy-start | bytes 393220
  76.9 7.6 %collective-permute-start.18 = (f32[3,32,1,128]{3,2,1,0:T(1,128)S(1)}, f32[3,32,1,128]{3,2,1,0:T(1,128)S(1)}, u32[]{:S(2)}, u32[]{:S(2)}) collective-permute-start(f32[3,32,1,128]{3,2,1,0:T(1,128)S(1)} %slice.746), channel_id=1, source_target_pairs={{0,1},{1,2},{2,3},{4,5},{5,6},{6,7},{8,9},{9,10},{10,11},{12,13},{... | collective-permute-start | bytes 147464 | tf_op jit(solution)/shard_map/ppermute | solution.py:20
  81.4 3.0 %collective-permute-start.19 = (f32[3,1,8,128]{3,2,1,0:T(8,128)S(1)}, f32[3,1,8,128]{3,2,1,0:T(8,128)S(1)}, u32[]{:S(2)}, u32[]{:S(2)}) collective-permute-start(f32[3,1,8,128]{3,2,1,0:T(8,128)S(1)} %slice.752), channel_id=1, source_target_pairs={{0,4},{1,5},{2,6},{3,7},{8,12},{9,13},{10,14},{11,15},{16,20},{17,... | collective-permute-start | bytes 36872 | tf_op jit(solution)/shard_map/ppermute | solution.py:20
  84.8 0.7 copy-start.8
  84.8 0.7 copy-start.11
  84.8 0.7 copy-start.14
  86.1 7.0 %collective-permute-start.20 = (f32[3,32,1,128]{3,2,1,0:T(1,128)}, f32[3,32,1,128]{3,2,1,0:T(1,128)}, u32[]{:S(2)}, u32[]{:S(2)}) collective-permute-start(f32[3,32,1,128]{3,2,1,0:T(1,128)} %slice.758), channel_id=1, source_target_pairs={{1,0},{2,1},{3,2},{5,4},{6,5},{7,6},{9,8},{10,9},{11,10},{13,12},{... | collective-permute-start | bytes 147464 | tf_op jit(solution)/shard_map/ppermute | solution.py:20
  87.4 5.7 %collective-permute-start.21 = (f32[3,1,8,128]{3,2,1,0:T(8,128)S(1)}, f32[3,1,8,128]{3,2,1,0:T(8,128)}, u32[]{:S(2)}, u32[]{:S(2)}) collective-permute-start(f32[3,1,8,128]{3,2,1,0:T(8,128)S(1)} %slice.764), channel_id=1, source_target_pairs={{4,0},{5,1},{6,2},{7,3},{12,8},{13,9},{14,10},{15,11},{20,16},{21,... | collective-permute-start | bytes 36872 | tf_op jit(solution)/shard_map/ppermute | solution.py:20
  90.3 2.8 %copy-start.9 = (f32[1,32,8,128]{3,2,1,0:T(8,128)S(1)}, f32[1,32,8,128]{3,2,1,0:T(8,128)}, u32[]{:S(2)}) copy-start(f32[1,32,8,128]{3,2,1,0:T(8,128)} %copy-done.8) | copy-start | bytes 393220
  90.3 2.8 %copy-start.12 = (f32[1,32,8,128]{3,2,1,0:T(8,128)S(1)}, f32[1,32,8,128]{3,2,1,0:T(8,128)}, u32[]{:S(2)}) copy-start(f32[1,32,8,128]{3,2,1,0:T(8,128)} %copy-done.11) | copy-start | bytes 393220
  90.3 2.8 %copy-start.15 = (f32[1,32,8,128]{3,2,1,0:T(8,128)S(1)}, f32[1,32,8,128]{3,2,1,0:T(8,128)}, u32[]{:S(2)}) copy-start(f32[1,32,8,128]{3,2,1,0:T(8,128)} %copy-done.14) | copy-start | bytes 393220
  90.3 2.8 %copy-start.18 = (f32[3,32,8]{2,1,0:T(8,128)S(1)}, f32[3,32,8]{2,1,0:T(8,128)}, u32[]{:S(2)}) copy-start(f32[3,32,8]{2,1,0:T(8,128)} %copy-done.17) | copy-start | bytes 9220
  90.3 2.8 %copy-start.21 = (f32[3,32,8]{2,1,0:T(8,128)S(1)}, f32[3,32,8]{2,1,0:T(8,128)}, u32[]{:S(2)}) copy-start(f32[3,32,8]{2,1,0:T(8,128)} %copy-done.20) | copy-start | bytes 9220
  94.3 0.9 copy-start.7
  95.2 8.0 %copy-start.5 = (f32[3,32,8,128]{3,2,1,0:T(8,128)S(1)}, f32[3,32,8,128]{3,2,1,0:T(8,128)}, u32[]{:S(2)}) copy-start(f32[3,32,8,128]{3,2,1,0:T(8,128)} %copy-done.4) | copy-start | bytes 1179652
  95.4 9.2 %collective-permute-start.22 = (f32[3,32,1,128]{3,2,1,0:T(1,128)S(1)}, f32[3,32,1,128]{3,2,1,0:T(1,128)S(1)}, u32[]{:S(2)}, u32[]{:S(2)}) collective-permute-start(f32[3,32,1,128]{3,2,1,0:T(1,128)S(1)} %slice.768), channel_id=1, source_target_pairs={{0,1},{1,2},{2,3},{4,5},{5,6},{6,7},{8,9},{9,10},{10,11},{12,13},{... | collective-permute-start | bytes 147464 | tf_op jit(solution)/shard_map/ppermute | solution.py:20
  100.0 4.7 %collective-permute-start.23 = (f32[3,1,8,128]{3,2,1,0:T(8,128)S(1)}, f32[3,1,8,128]{3,2,1,0:T(8,128)S(1)}, u32[]{:S(2)}, u32[]{:S(2)}) collective-permute-start(f32[3,1,8,128]{3,2,1,0:T(8,128)S(1)} %slice.774), channel_id=1, source_target_pairs={{0,4},{1,5},{2,6},{3,7},{8,12},{9,13},{10,14},{11,15},{16,20},{17,... | collective-permute-start | bytes 36872 | tf_op jit(solution)/shard_map/ppermute | solution.py:20
  104.9 0.9 copy-start.23
  104.9 0.9 copy-start.25
  105.0 0.8 copy-start.28
  106.4 6.3 %copy-start.16 = (f32[1,32,8,128]{3,2,1,0:T(8,128)S(1)}, f32[1,32,8,128]{3,2,1,0:T(8,128)}, u32[]{:S(2)}) copy-start(f32[1,32,8,128]{3,2,1,0:T(8,128)} %copy-done.14) | copy-start | bytes 393220
  106.5 6.3 %copy-start.22 = (f32[3,32,8]{2,1,0:T(8,128)S(1)}, f32[3,32,8]{2,1,0:T(8,128)}, u32[]{:S(2)}) copy-start(f32[3,32,8]{2,1,0:T(8,128)} %copy-done.20) | copy-start | bytes 9220
  106.6 6.2 %copy-start.13 = (f32[1,32,8,128]{3,2,1,0:T(8,128)S(1)}, f32[1,32,8,128]{3,2,1,0:T(8,128)}, u32[]{:S(2)}) copy-start(f32[1,32,8,128]{3,2,1,0:T(8,128)} %copy-done.11) | copy-start | bytes 393220
  112.1 0.9 copy-start.10
  112.1 0.9 copy-start.19
